TPU v7x, 32 devices: a whole 2x2x4 slice. The times are simulated.
32 devices in a mesh: arrays: 2 (over y), tm: 8 (over z, x), chan: 2 (over core).
Axes of the slice: x: 2, y: 2, z: 4, core: 2. Of those that a mesh axis runs over, the one named last changes fastest.
Arguments:
- spectra: bfloat16 [128, 256, 2, 128], P(('arrays', 'tm'), 'chan'), parts along dimension 0, may hold values from -40 to 40
- offsets: int32 [128], P(('arrays', 'tm')), parts along dimension 0, may hold values from 0 to 63
- channel_group: int32 [512], P(('arrays', 'chan')), parts along dimension 0, may hold values from 0 to 7
Outputs:
- stack: float32 [128, 48, 128], P(('arrays', 'tm', 'chan')), parts along dimension 0
There are 2 independent parts, one for each index of `arrays`. A program takes and returns all parts, laid end to end along the dimension named above; each array names one. Nothing has to cross between parts.
All inputs are finite; a program needn't handle non-finite values.
Results may differ from a plain program's by a relative error of at most 0.0075.
Values may be sent and summed in bfloat16 or wider, within the bound.
A program may use at most 64 MiB of HBM per device.

v0:
```python
import functools
import math

import jax
import jax.numpy as jnp
from jax import lax
from jax.experimental import pallas as pl
from jax.experimental.pallas import tpu as pltpu
from jax.sharding import PartitionSpec as P

LAGS = 128
GROUPS = 8
SPAN = 6


epsilon = 1e-05


def shifted(value, axis, steps):
    count = lax.axis_size(axis)
    initial, last = (max(0, -steps), min(count, count - steps))
    return lax.ppermute(value, axis, [(source, source + steps) for source in range(initial, last)])


def lag_table(freq_bins, lag_count):
    frequency = jnp.arange(freq_bins, dtype=jnp.int32)[:, None]
    lag_shift = jnp.arange(lag_count, dtype=jnp.int32)[None, :] - lag_count // 2
    phase_turns = jnp.mod(frequency * lag_shift, 2 * freq_bins).astype(jnp.float32)
    phase_angle = jnp.pi * phase_turns / freq_bins
    normaliser = 1.0 / math.sqrt(freq_bins)
    lag_rows = jnp.concatenate(
        [jnp.cos(phase_angle) * normaliser, -jnp.sin(phase_angle) * normaliser], axis=0
    )
    return lag_rows.astype(jnp.bfloat16)


def align_spectra(spectra, offsets, scales):
    freq_bins = spectra.shape[3]
    frequency = jnp.arange(freq_bins, dtype=jnp.int32)[None, :]
    phase_turns = jnp.mod(offsets[:, None] * frequency, 2 * freq_bins).astype(jnp.float32)
    phase_angle = jnp.pi * phase_turns / freq_bins
    cosine = jnp.cos(phase_angle)[:, None, :]
    sine_part = jnp.sin(phase_angle)[:, None, :]
    real_part = spectra[:, :, 0, :].astype(jnp.float32)
    imag_part = spectra[:, :, 1, :].astype(jnp.float32)
    weight = scales[:, :, None]
    out_real = weight * (real_part * cosine + imag_part * sine_part)
    out_imag = weight * (imag_part * cosine - real_part * sine_part)
    return jnp.stack([out_real, out_imag], axis=2).astype(jnp.bfloat16)


def window_terms(current, band_rows, lag_rows):
    left_real = current[None, :, 0, :].astype(jnp.float32)
    left_imag = current[None, :, 1, :].astype(jnp.float32)
    right_real = band_rows[:, :, 0, :].astype(jnp.float32)
    right_imag = band_rows[:, :, 1, :].astype(jnp.float32)
    prod_real = left_real * right_real + left_imag * right_imag
    prod_imag = left_imag * right_real - left_real * right_imag
    cross_spec = jnp.stack([prod_real, prod_imag], axis=2).astype(jnp.bfloat16)
    flattened = cross_spec.reshape(band_rows.shape[0] * band_rows.shape[1], 2 * band_rows.shape[3])
    lagged = jnp.dot(flattened, lag_rows, preferred_element_type=jnp.float32)
    lagged = lagged.reshape(band_rows.shape[0], band_rows.shape[1], lag_rows.shape[1])
    return jnp.sum(lagged * lagged, axis=1)


def ring_shards(spectra, offsets, channel_group):
    windows = spectra.shape[0]
    local_chans = spectra.shape[1]
    freq_bins = spectra.shape[3]
    chan_count = lax.axis_size("chan")
    channels = local_chans * chan_count
    onehot = (channel_group[:, None] == jnp.arange(GROUPS, dtype=jnp.int32)[None, :]).astype(
        jnp.float32
    )
    chan_power = jnp.sum(jnp.square(spectra.astype(jnp.float32)), axis=(2, 3))
    partial_value = jnp.dot(chan_power, onehot, precision=lax.Precision.HIGHEST)
    group_total = lax.psum(partial_value, "chan")
    energy = group_total * (GROUPS / (freq_bins * channels))
    scales = jnp.dot(lax.rsqrt(energy + epsilon), onehot.T, precision=lax.Precision.HIGHEST)
    aligned = align_spectra(spectra, offsets, scales)
    earlier = []
    carried = aligned
    for distance in range(SPAN):
        carried = shifted(carried, "tm", 1)
        earlier.append(carried)
    buffer = jnp.concatenate(earlier[::-1] + [aligned], axis=0)
    lag_rows = lag_table(freq_bins, LAGS)
    band_len = SPAN * windows

    def one_window(window):
        current = lax.dynamic_index_in_dim(aligned, window, 0, keepdims=False)
        band_rows = lax.dynamic_slice_in_dim(buffer, window, band_len, 0)
        return window_terms(current, band_rows, lag_rows) * (1.0 / channels)

    return lax.psum_scatter(
        lax.map(
            one_window, jnp.arange(lax.axis_size("chan") * (windows // chan_count), dtype=jnp.int32)
        ).astype(jnp.bfloat16),
        "chan",
        scatter_dimension=0,
        tiled=True,
    ).astype(jnp.float32)


LATE = 4
HIGHEST = lax.Precision.HIGHEST


def phase_of(turns, freq_bins):
    period = 2.0 * freq_bins
    return (jnp.pi / freq_bins) * (turns - period * jnp.floor(turns / period))


def kernel(
    n, chans, windows, share, freq_bins, cores,
    x_ref, off_ref, group_ref, out_ref,
    local, wide, raw, unpacked, tile, tiles, table, right, left, part, half_out, half_in, sum_out, sum_in,
    local_sem, keep_sem, x_send, x_recv, e_send, e_recv, h_send, h_recv, s_send, s_recv,
):
    me = lax.axis_index("tm")
    core = lax.axis_index("chan")
    band = SPAN * windows
    mine = windows // cores
    lanes = freq_bins

    load = pltpu.make_async_copy(x_ref, local, local_sem)
    load.start()
    keep = pltpu.make_async_copy(x_ref.at[:, pl.ds(me * 2 * share, 2 * share), :], raw.at[me], keep_sem)
    keep.start()

    barrier = pltpu.get_barrier_semaphore()
    for d in range(n):
        for k in range(cores):
            if d or k:
                pl.semaphore_signal(
                    barrier, inc=1,
                    device_id={"tm": lax.rem(me + d, n), "chan": lax.rem(core + k, cores)},
                    device_id_type=pl.DeviceIdType.MESH,
                )
    def x_copy(there, slot):
        return pltpu.make_async_remote_copy(
            src_ref=x_ref.at[:, pl.ds(there * 2 * share, 2 * share), :],
            dst_ref=raw.at[slot],
            send_sem=x_send.at[there],
            recv_sem=x_recv.at[slot],
            device_id={"tm": there},
            device_id_type=pl.DeviceIdType.MESH,
        )

    load.wait()
    for w in range(windows):
        wide[pl.ds(w * 2 * chans, 2 * chans), :] = local[w].astype(jnp.float32)
    lane = lax.broadcasted_iota(jnp.int32, (windows, lanes), 1)
    row = lax.broadcasted_iota(jnp.int32, (windows, lanes), 0)

    def power_step(c, held):
        real = wide[pl.ds(2 * c, windows, stride=2 * chans), :]
        imag = wide[pl.ds(2 * c + 1, windows, stride=2 * chans), :]
        power = jnp.sum(real * real + imag * imag, axis=1, keepdims=True)
        return jnp.where(lane == c, power, held)

    chan_power = lax.fori_loop(0, chans, power_step, jnp.zeros((windows, lanes), jnp.float32), unroll=8)
    group_id = lax.broadcasted_iota(jnp.int32, (lanes, chans), 0)
    onehot = (group_id == group_ref[...]).astype(jnp.float32)
    totals = lax.dot_general(
        chan_power, onehot, (((1,), (1,)), ((), ())), precision=HIGHEST, preferred_element_type=jnp.float32
    )
    for w in range(windows):
        totals = jnp.where((lane == lanes - 1) & (row == w), off_ref[w].astype(jnp.float32), totals)
    tile[...] = totals

    def e_copy(there, other, slot):
        return pltpu.make_async_remote_copy(
            src_ref=tile,
            dst_ref=tiles.at[slot],
            send_sem=e_send.at[there * cores + other],
            recv_sem=e_recv.at[slot],
            device_id={"tm": there, "chan": other},
            device_id_type=pl.DeviceIdType.MESH,
        )

    def others():
        for d in range(n):
            for k in range(cores):
                if d or k:
                    yield lax.rem(me + d, n), lax.rem(core + k, cores)

    pl.semaphore_wait(barrier, n * cores - 1)
    for there, other in others():
        e_copy(there, other, me * cores + core).start()
    for d in range(1, n):
        x_copy(lax.rem(me + d, n), me).start()
    tiles[me * cores + core] = totals

    frequency = lax.broadcasted_iota(jnp.int32, (freq_bins, LAGS), 0)
    shift = lax.broadcasted_iota(jnp.int32, (freq_bins, LAGS), 1) - LAGS // 2
    angle = phase_of((frequency * shift).astype(jnp.float32), freq_bins)
    normaliser = 1.0 / math.sqrt(freq_bins)
    table[pl.ds(0, freq_bins), :] = (jnp.cos(angle) * normaliser).astype(jnp.bfloat16)
    table[pl.ds(freq_bins, freq_bins), :] = (-jnp.sin(angle) * normaliser).astype(jnp.bfloat16)
    part[...] = jnp.zeros_like(part)

    my_onehot = (group_id == pltpu.roll(group_ref[...], lax.rem(chans - me * share, chans), 1)).astype(jnp.float32)
    bins = lax.broadcasted_iota(jnp.int32, (windows, freq_bins), 1).astype(jnp.float32)
    keep.wait()
    for there, other in others():
        e_copy(there, other, there * cores + other).wait_recv()

    early = n - LATE

    def pair_block(t, s):
        for j in range(windows):
            w = t * windows + j
            rows = [left[w, c, 0] * right[c, 0, s] + left[w, c, 1] * right[c, 1, s] for c in range(share)]
            lagged = jnp.dot(jnp.concatenate(rows, axis=0), table[...], preferred_element_type=jnp.float32)
            lagged = lagged.reshape(share, windows, LAGS)
            place = band + windows + s * windows - w
            part[w, pl.ds(place, windows), :] = jnp.sum(lagged * lagged, axis=0)

    def align_step(i, carry):
        t = lax.rem(me + n - i, n)

        @pl.when(i > 0)
        def _():
            x_copy(t, t).wait_recv()

        for w in range(windows):
            unpacked[pl.ds(w * 2 * share, 2 * share), :] = raw[t, w].astype(jnp.float32)
        first = tiles[t * cores]
        summed = first
        for k in range(1, cores):
            summed = summed + tiles[t * cores + k]
        energy = summed * (GROUPS / (freq_bins * chans * cores))
        scales = jnp.dot(
            lax.rsqrt(energy + epsilon), my_onehot, precision=HIGHEST, preferred_element_type=jnp.float32
        )
        theta = phase_of(bins * first[:, lanes - 1 : lanes], freq_bins)
        cosine = jnp.cos(theta)
        sine = jnp.sin(theta)
        for c in range(share):
            real = unpacked[pl.ds(2 * c, windows, stride=2 * share), :]
            imag = unpacked[pl.ds(2 * c + 1, windows, stride=2 * share), :]
            weight = scales[:, c : c + 1]
            out_real = weight * (real * cosine + imag * sine)
            out_imag = weight * (imag * cosine - real * sine)
            right[c, 0, t] = jnp.concatenate([out_real, out_imag], axis=1).astype(jnp.bfloat16)
            right[c, 1, t] = jnp.concatenate([out_imag, out_real], axis=1).astype(jnp.bfloat16)
            for j in range(windows):
                one_real = jnp.broadcast_to(out_real[j : j + 1, :], (windows, freq_bins))
                one_imag = jnp.broadcast_to(out_imag[j : j + 1, :], (windows, freq_bins))
                w = t * windows + j
                left[w, c, 0] = jnp.concatenate([one_real, -one_real], axis=1).astype(jnp.bfloat16)
                left[w, c, 1] = jnp.concatenate([one_imag, one_imag], axis=1).astype(jnp.bfloat16)

        def known_pair(k, held):
            other = lax.rem(me + n - k, n)
            upper, lower = jnp.maximum(t, other), jnp.minimum(t, other)

            @pl.when(upper - lower <= SPAN)
            def _():
                pair_block(upper, lower)

            return held

        @pl.when(i < early)
        def _():
            lax.fori_loop(0, i + 1, known_pair, 0)

        return carry

    lax.fori_loop(0, n, align_step, 0)

    def h_copy(t):
        return pltpu.make_async_remote_copy(
            src_ref=half_out.at[t],
            dst_ref=half_in.at[t],
            send_sem=h_send.at[t],
            recv_sem=h_recv.at[t],
            device_id={"chan": 1 - core},
            device_id_type=pl.DeviceIdType.MESH,
        )

    def s_copy(t, slot):
        return pltpu.make_async_remote_copy(
            src_ref=sum_out.at[t],
            dst_ref=sum_in.at[slot],
            send_sem=s_send.at[t],
            recv_sem=s_recv.at[slot],
            device_id={"tm": t},
            device_id_type=pl.DeviceIdType.MESH,
        )

    def pass_on(t):
        h_copy(t).wait_recv()
        return part[pl.ds(t * windows + core * mine, mine), pl.ds(windows, band), :] + half_in[t].astype(jnp.float32)

    def stage(i, carry):
        t = lax.rem(me + 1 + i, n)

        def one_block(s, held):
            behind = jnp.maximum(lax.rem(me - t + n, n), lax.rem(me - s + n, n))

            @pl.when(behind >= early)
            def _():
                pair_block(t, s)

            return held

        lax.fori_loop(jnp.maximum(t - SPAN, 0), t + 1, one_block, 0)
        half_out[t] = part[pl.ds(t * windows + (1 - core) * mine, mine), pl.ds(windows, band), :].astype(jnp.bfloat16)
        h_copy(t).start()

        @pl.when(i > 0)
        def _():
            before = lax.rem(me + i, n)
            sum_out[before] = pass_on(before).astype(jnp.bfloat16)
            s_copy(before, me).start()

        return carry

    lax.fori_loop(0, n, stage, 0)
    result = pass_on(me)
    for d in range(1, n):
        s = lax.rem(me + n - d, n)
        s_copy(s, s).wait_recv()
        result = result + sum_in[s].astype(jnp.float32)
    out_ref[...] = result * (1.0 / (chans * cores))

    for d in range(1, n):
        t = lax.rem(me + d, n)
        x_copy(t, me).wait_send()
        s_copy(t, me).wait_send()
    for t in range(n):
        h_copy(t).wait_send()
    for there, other in others():
        e_copy(there, other, me * cores + core).wait_send()


def spread_shards(spectra, offsets, channel_group):
    windows, chans, _, freq_bins = spectra.shape
    n = lax.axis_size("tm")
    cores = lax.axis_size("chan")
    share = chans // n
    total = n * windows
    band = SPAN * windows
    mine = windows // cores
    dma = pltpu.SemaphoreType.DMA
    return pl.pallas_call(
        functools.partial(kernel, n, chans, windows, share, freq_bins, cores),
        out_shape=jax.ShapeDtypeStruct((mine, band, LAGS), jnp.float32),
        in_specs=[
            pl.BlockSpec(memory_space=pl.ANY),
            pl.BlockSpec(memory_space=pltpu.SMEM),
            pl.BlockSpec(memory_space=pltpu.VMEM),
        ],
        out_specs=pl.BlockSpec(memory_space=pltpu.VMEM),
        scratch_shapes=[
            pltpu.VMEM((windows, 2 * chans, freq_bins), jnp.bfloat16),
            pltpu.VMEM((windows * 2 * chans, freq_bins), jnp.float32),
            pltpu.VMEM((n, windows, 2 * share, freq_bins), jnp.bfloat16),
            pltpu.VMEM((windows * 2 * share, freq_bins), jnp.float32),
            pltpu.VMEM((windows, freq_bins), jnp.float32),
            pltpu.VMEM((n * cores, windows, freq_bins), jnp.float32),
            pltpu.VMEM((2 * freq_bins, LAGS), jnp.bfloat16),
            pltpu.VMEM((share, 2, n, windows, 2 * freq_bins), jnp.bfloat16),
            pltpu.VMEM((total, share, 2, windows, 2 * freq_bins), jnp.bfloat16),
            pltpu.VMEM((total, band + 2 * windows, LAGS), jnp.float32),
            pltpu.VMEM((n, mine, band, LAGS), jnp.bfloat16),
            pltpu.VMEM((n, mine, band, LAGS), jnp.bfloat16),
            pltpu.VMEM((n, mine, band, LAGS), jnp.bfloat16),
            pltpu.VMEM((n, mine, band, LAGS), jnp.bfloat16),
            dma, dma, dma((n,)), dma((n,)), dma((n * cores,)), dma((n * cores,)),
            dma((n,)), dma((n,)), dma((n,)), dma((n,)),
        ],
        compiler_params=pltpu.CompilerParams(
            collective_id=0, has_side_effects=True, vmem_limit_bytes=56 * 1024 * 1024
        ),
    )(spectra.reshape(windows, 2 * chans, freq_bins), offsets, channel_group.reshape(1, chans))


def shards(spectra, offsets, channel_group):
    windows, chans, _, freq_bins = spectra.shape
    n = lax.axis_size("tm")
    fits = (
        chans == freq_bins == LAGS == 128
        and windows == 8
        and lax.axis_size("chan") == 2
        and chans % n == 0
        and chans // n >= 8
    )
    return (spread_shards if fits else ring_shards)(spectra, offsets, channel_group)


def solution(mesh):
    placed = (P(("arrays", "tm"), "chan", None, None), P(("arrays", "tm")), P(("arrays", "chan")))
    return jax.shard_map(
        shards,
        mesh=mesh,
        in_specs=placed,
        out_specs=P(("arrays", "tm", "chan"), None, None),
        check_vma=False,
    )
```

profile of v0, /device:TPU:11, one launch (start us, length us, event | category | flops | bytes accessed | tf_op | source)
XLA Modules:
  0.0 38.7 jit_solution(14963574788099180043)
XLA Ops:
  0.0 37.2 %shard_map.37 = f32[4,48,128]{2,1,0:T(8,128)} custom-call(bf16[8,256,128]{2,1,0:T(8,128)(2,1)} %bitcast.2, s32[8]{0:T(128)} %off_ref.1, s32[1,128]{1,0:T(1,128)} %bitcast.3), custom_call_target="tpu_custom_call" | custom-call | tf_op jit(solution)/shard_map/pallas_call | solution.py:348
  37.2 1.5 %copy.5 = f32[4,48,128]{2,1,0:T(8,128)} copy(f32[4,48,128]{2,1,0:T(8,128)} %shard_map.37) | data formatting | bytes 196608
where the time goes:
time: 38.9 us; the launch traced here: 38.7 us
  Pallas kernels  37.2 us (96%)
  local copies, waits for them, and re-layouts  1.54 us (4%)
    pallas_call x1, Pallas kernels, spread_shards(): pl.pallas_call(functools.partial(kernel, n, chans, windows, share, freq_b...  37.2 us
    unnamed x1, local copies, waits for them, and re-layouts  1.54 us

commit v1 on v0

v1 whole, which is shorter than its diff:
```python
import functools
import math

import jax
import jax.numpy as jnp
from jax import lax
from jax.experimental import pallas as pl
from jax.experimental.pallas import tpu as pltpu
from jax.sharding import PartitionSpec as P

LAGS = 128
GROUPS = 8
SPAN = 6


epsilon = 1e-05


def shifted(value, axis, steps):
    count = lax.axis_size(axis)
    initial, last = (max(0, -steps), min(count, count - steps))
    return lax.ppermute(value, axis, [(source, source + steps) for source in range(initial, last)])


def lag_table(freq_bins, lag_count):
    frequency = jnp.arange(freq_bins, dtype=jnp.int32)[:, None]
    lag_shift = jnp.arange(lag_count, dtype=jnp.int32)[None, :] - lag_count // 2
    phase_turns = jnp.mod(frequency * lag_shift, 2 * freq_bins).astype(jnp.float32)
    phase_angle = jnp.pi * phase_turns / freq_bins
    normaliser = 1.0 / math.sqrt(freq_bins)
    lag_rows = jnp.concatenate(
        [jnp.cos(phase_angle) * normaliser, -jnp.sin(phase_angle) * normaliser], axis=0
    )
    return lag_rows.astype(jnp.bfloat16)


def align_spectra(spectra, offsets, scales):
    freq_bins = spectra.shape[3]
    frequency = jnp.arange(freq_bins, dtype=jnp.int32)[None, :]
    phase_turns = jnp.mod(offsets[:, None] * frequency, 2 * freq_bins).astype(jnp.float32)
    phase_angle = jnp.pi * phase_turns / freq_bins
    cosine = jnp.cos(phase_angle)[:, None, :]
    sine_part = jnp.sin(phase_angle)[:, None, :]
    real_part = spectra[:, :, 0, :].astype(jnp.float32)
    imag_part = spectra[:, :, 1, :].astype(jnp.float32)
    weight = scales[:, :, None]
    out_real = weight * (real_part * cosine + imag_part * sine_part)
    out_imag = weight * (imag_part * cosine - real_part * sine_part)
    return jnp.stack([out_real, out_imag], axis=2).astype(jnp.bfloat16)


def window_terms(current, band_rows, lag_rows):
    left_real = current[None, :, 0, :].astype(jnp.float32)
    left_imag = current[None, :, 1, :].astype(jnp.float32)
    right_real = band_rows[:, :, 0, :].astype(jnp.float32)
    right_imag = band_rows[:, :, 1, :].astype(jnp.float32)
    prod_real = left_real * right_real + left_imag * right_imag
    prod_imag = left_imag * right_real - left_real * right_imag
    cross_spec = jnp.stack([prod_real, prod_imag], axis=2).astype(jnp.bfloat16)
    flattened = cross_spec.reshape(band_rows.shape[0] * band_rows.shape[1], 2 * band_rows.shape[3])
    lagged = jnp.dot(flattened, lag_rows, preferred_element_type=jnp.float32)
    lagged = lagged.reshape(band_rows.shape[0], band_rows.shape[1], lag_rows.shape[1])
    return jnp.sum(lagged * lagged, axis=1)


def ring_shards(spectra, offsets, channel_group):
    windows = spectra.shape[0]
    local_chans = spectra.shape[1]
    freq_bins = spectra.shape[3]
    chan_count = lax.axis_size("chan")
    channels = local_chans * chan_count
    onehot = (channel_group[:, None] == jnp.arange(GROUPS, dtype=jnp.int32)[None, :]).astype(
        jnp.float32
    )
    chan_power = jnp.sum(jnp.square(spectra.astype(jnp.float32)), axis=(2, 3))
    partial_value = jnp.dot(chan_power, onehot, precision=lax.Precision.HIGHEST)
    group_total = lax.psum(partial_value, "chan")
    energy = group_total * (GROUPS / (freq_bins * channels))
    scales = jnp.dot(lax.rsqrt(energy + epsilon), onehot.T, precision=lax.Precision.HIGHEST)
    aligned = align_spectra(spectra, offsets, scales)
    earlier = []
    carried = aligned
    for distance in range(SPAN):
        carried = shifted(carried, "tm", 1)
        earlier.append(carried)
    buffer = jnp.concatenate(earlier[::-1] + [aligned], axis=0)
    lag_rows = lag_table(freq_bins, LAGS)
    band_len = SPAN * windows

    def one_window(window):
        current = lax.dynamic_index_in_dim(aligned, window, 0, keepdims=False)
        band_rows = lax.dynamic_slice_in_dim(buffer, window, band_len, 0)
        return window_terms(current, band_rows, lag_rows) * (1.0 / channels)

    return lax.psum_scatter(
        lax.map(
            one_window, jnp.arange(lax.axis_size("chan") * (windows // chan_count), dtype=jnp.int32)
        ).astype(jnp.bfloat16),
        "chan",
        scatter_dimension=0,
        tiled=True,
    ).astype(jnp.float32)


HIGHEST = lax.Precision.HIGHEST
PAIR = 2
COLUMNS = 2
PARTS = 4


def phase_of(turns, freq_bins):
    period = 2.0 * freq_bins
    return (jnp.pi / freq_bins) * (turns - period * jnp.floor(turns / period))


def kernel(
    n, chans, windows, freq_bins, cores,
    x_ref, off_ref, group_ref, out_ref,
    local, wide, sums, tile, tile_in, al, right, left, table, acc, total, sum_out, sum_in,
    local_sem, own_sem, e_send, e_recv, x_send, x_recv, f_send, f_recv, s_send, s_recv, ready,
):
    me = lax.axis_index("tm")
    core = lax.axis_index("chan")
    levels = n // COLUMNS
    level, column = me // COLUMNS, lax.rem(me, COLUMNS)
    half = level // 2
    inner = jnp.logical_or(level == 1, level == levels - 2)
    blocks = n // 2
    mine = windows // cores
    lanes = freq_bins
    bf16 = jnp.bfloat16
    groups = chans // windows
    chunk = groups // PARTS
    pairs = windows // PAIR
    mesh_id = pl.DeviceIdType.MESH

    load = pltpu.make_async_copy(x_ref, local, local_sem)
    load.start()

    barrier = pltpu.get_barrier_semaphore()
    beside = COLUMNS * level + 1 - column
    above, below = level + 1 < levels, level > 0

    def greet(sem):
        pl.semaphore_signal(sem, inc=1, device_id={"tm": beside}, device_id_type=mesh_id)

        @pl.when(above)
        def _():
            pl.semaphore_signal(sem, inc=1, device_id={"tm": me + COLUMNS}, device_id_type=mesh_id)

        @pl.when(below)
        def _():
            pl.semaphore_signal(sem, inc=1, device_id={"tm": me - COLUMNS}, device_id_type=mesh_id)

    near = 1 + jnp.where(above, 1, 0) + jnp.where(below, 1, 0)
    pl.semaphore_signal(barrier, inc=1, device_id={"chan": 1 - core}, device_id_type=mesh_id)
    greet(barrier)

    frequency = lax.broadcasted_iota(jnp.int32, (freq_bins, LAGS), 0)
    shift = lax.broadcasted_iota(jnp.int32, (freq_bins, LAGS), 1) - LAGS // 2
    group_id = lax.broadcasted_iota(jnp.int32, (lanes, chans), 0)
    onehot = (group_id == group_ref[...]).astype(jnp.float32)
    few = onehot[:GROUPS].astype(bf16)
    both = jnp.concatenate([few, few], axis=1)
    lane = lax.broadcasted_iota(jnp.int32, (windows, lanes), 1)
    row = lax.broadcasted_iota(jnp.int32, (windows, lanes), 0)

    load.wait()
    for w in range(windows):
        wide[pl.ds(w * 2 * chans, 2 * chans), :] = local[w].astype(jnp.float32)
    for w in range(windows):
        real = wide[pl.ds(w * 2 * chans, chans, stride=2), :]
        imag = wide[pl.ds(w * 2 * chans + 1, chans, stride=2), :]
        power = real * real + imag * imag
        high = power.astype(bf16)
        low = (power - high.astype(jnp.float32)).astype(bf16)
        sums[pl.ds(w * GROUPS, GROUPS), :] = jnp.dot(
            both, jnp.concatenate([high, low], axis=0), preferred_element_type=jnp.float32
        )
    totals = jnp.zeros((windows, lanes), jnp.float32)
    for g in range(GROUPS):
        held = jnp.sum(sums[pl.ds(g, windows, stride=GROUPS), :], axis=1, keepdims=True)
        totals = jnp.where(lane == g, held, totals)
    tile[...] = totals
    e_copy = pltpu.make_async_remote_copy(
        src_ref=tile, dst_ref=tile_in, send_sem=e_send, recv_sem=e_recv,
        device_id={"chan": 1 - core}, device_id_type=mesh_id,
    )
    pl.semaphore_wait(barrier, near + 1)
    e_copy.start()
    greet(ready.at[0])

    angle = phase_of((frequency * shift).astype(jnp.float32), freq_bins)
    normaliser = 1.0 / math.sqrt(freq_bins)
    table[pl.ds(0, freq_bins), :] = (jnp.cos(angle) * normaliser).astype(bf16)
    table[pl.ds(freq_bins, freq_bins), :] = (-jnp.sin(angle) * normaliser).astype(bf16)
    starts = jnp.zeros((windows, lanes), jnp.float32)
    for w in range(windows):
        starts = jnp.where(row == w, off_ref[w].astype(jnp.float32), starts)
    theta = phase_of(lane.astype(jnp.float32) * starts, freq_bins)
    cosine = jnp.cos(theta)
    sine = jnp.sin(theta)
    acc[...] = jnp.zeros_like(acc)
    total[:, pl.ds(0, SPAN * windows), :] = jnp.zeros((mine, SPAN * windows, LAGS), jnp.float32)

    pl.semaphore_wait(ready.at[0], near)
    greet(ready.at[1])
    e_copy.wait_recv()
    energy = (totals + tile_in[...]) * (GROUPS / (freq_bins * chans * cores))
    scales = jnp.dot(lax.rsqrt(energy + epsilon), onehot, precision=HIGHEST, preferred_element_type=jnp.float32)

    def aligned(c):
        real = wide[pl.ds(2 * c, windows, stride=2 * chans), :]
        imag = wide[pl.ds(2 * c + 1, windows, stride=2 * chans), :]
        weight = scales[:, c : c + 1]
        return weight * (real * cosine + imag * sine), weight * (imag * cosine - real * sine)

    for g in range(groups):
        for p in range(pairs):
            one, two = (aligned((g * pairs + p) * PAIR + i) for i in range(PAIR))
            for r in range(2):
                al[g, 2 * p + r] = jnp.concatenate([one[r], two[r]], axis=0).astype(bf16)
    pl.semaphore_wait(ready.at[1], near)

    def routes():
        for own in (1, 0):
            for flip in range(COLUMNS):
                place = COLUMNS * jnp.where(own == 1, half, 1 - half) + (column if flip == 0 else 1 - column)
                yield COLUMNS + place, chunk * place, 0, 2 * (1 - own) + flip
        for part in range(2):
            for flip in range(COLUMNS):
                place = column if flip == 0 else 1 - column
                yield (n - COLUMNS) * half + place, chunk * (2 * place + part), part, 4 + 2 * part + flip

    def slot(part, of):
        return (part * cores + of) * chunk

    def x_copy(there, first, part, index, source):
        return pltpu.make_async_remote_copy(
            src_ref=al.at[pl.ds(first, chunk)],
            dst_ref=right.at[source, pl.ds(slot(part, core), chunk)],
            send_sem=x_send.at[index],
            recv_sem=x_recv.at[source, part],
            device_id={"tm": there},
            device_id_type=mesh_id,
        )

    def own_copy(first, part):
        return pltpu.make_async_copy(
            al.at[pl.ds(first, chunk)], right.at[me, pl.ds(slot(part, core), chunk)], own_sem.at[part]
        )

    def f_copy(t, part):
        return pltpu.make_async_remote_copy(
            src_ref=right.at[t, pl.ds(slot(part, core), chunk)],
            dst_ref=right.at[t, pl.ds(slot(part, core), chunk)],
            send_sem=f_send.at[t, part],
            recv_sem=f_recv.at[t, part],
            device_id={"chan": 1 - core},
            device_id_type=mesh_id,
        )

    for there, first, part, index in routes():
        @pl.when(there == me)
        def _():
            own_copy(first, part).start()

        @pl.when(there != me)
        def _():
            x_copy(there, first, part, index, me).start()

    bit = lax.rem(level, 2)

    def block(base, flip, k):
        return base + COLUMNS * lax.rem(bit + flip + k // 2, 2) + lax.rem(column + lax.rem(k, 2), 2)

    here, away = blocks * half, blocks * (1 - half)

    def job(upper, lower, first):
        up, low = lax.rem(upper, blocks), lax.rem(lower, blocks)
        for j in range(mine):
            rows = []
            at = core * mine + j
            for g in range(chunk):
                for p in range(pairs):
                    right_real = right[lower, first + g, 2 * p]
                    right_imag = right[lower, first + g, 2 * p + 1]
                    picked = [
                        jnp.concatenate(
                            [left[upper, first + g, 2 * p + r, pl.ds(i * windows + at, windows, stride=0), :] for i in range(PAIR)],
                            axis=0,
                        ).astype(bf16)
                        for r in range(2)
                    ]
                    left_real, left_imag = picked
                    rows.append(
                        jnp.concatenate(
                            [
                                left_real * right_real + left_imag * right_imag,
                                left_imag * right_real - left_real * right_imag,
                            ],
                            axis=1,
                        )
                    )
            lagged = jnp.dot(jnp.concatenate(rows, axis=0), table[...], preferred_element_type=jnp.float32)
            lagged = lagged.reshape(chunk * pairs * PAIR, windows, LAGS)
            acc[up, j, pl.ds(low * windows, windows), :] += jnp.sum(lagged * lagged, axis=0)

    holder = jnp.where(inner, me - COLUMNS, 2 * COLUMNS + column)
    target = blocks * jnp.where(inner, 1, half)

    def s_copy(local_t, source):
        return pltpu.make_async_remote_copy(
            src_ref=sum_out.at[local_t],
            dst_ref=sum_in.at[source],
            send_sem=s_send.at[local_t],
            recv_sem=s_recv.at[source],
            device_id={"tm": target + local_t},
            device_id_type=mesh_id,
        )

    def hand_over(local_t):
        @pl.when(target + local_t == me)
        def _():
            sum_in[holder] = acc[local_t].astype(bf16)

        @pl.when(target + local_t != me)
        def _():
            sum_out[local_t] = acc[local_t].astype(bf16)
            s_copy(local_t, holder).start()

    early = jnp.logical_and(inner, half == 0)

    def step(q, carry):
        part = jnp.where(inner, 0, q // blocks)
        i = lax.rem(q, blocks)
        far = jnp.logical_and(inner, q >= blocks)
        t = jnp.where(far, block(away, 1, i), block(here, 0, i))
        count = jnp.where(inner, jnp.where(far, blocks, 0), i + 1)

        @pl.when(t == me)
        def _():
            own_copy(0, part).wait()

        @pl.when(t != me)
        def _():
            x_copy(me, 0, part, 0, t).wait_recv()

        f_copy(t, part).start()

        def one_side(c, held):
            first = slot(part, lax.rem(core + c, cores))

            @pl.when(c > 0)
            def _():
                f_copy(t, part).wait_recv()

            for g in range(chunk):
                for r in range(2 * pairs):
                    left[t, first + g, r] = right[t, first + g, r].astype(jnp.float32)

            def one_job(k, inside):
                other = block(here, 0, k)
                upper, lower = jnp.maximum(t, other), jnp.minimum(t, other)

                @pl.when(upper - lower <= SPAN)
                def _():
                    job(upper, lower, first)

                return inside

            lax.fori_loop(0, count, one_job, 0)
            return held

        lax.fori_loop(0, cores, one_side, 0)

        @pl.when(jnp.logical_and(early, far))
        def _():
            hand_over(lax.rem(t, blocks))

        return carry

    lax.fori_loop(0, n, step, 0)

    @pl.when(jnp.logical_not(early))
    def _():
        for local_t in range(blocks):
            hand_over(local_t)

    def collect(first, count):
        result = None
        for source in range(first, first + count):
            @pl.when(source != holder_here)
            def _():
                s_copy(0, source).wait_recv()

            value = sum_in[source].astype(jnp.float32)
            result = value if result is None else result + value
        return result

    keeps = jnp.logical_and(me >= target, me < target + blocks)
    holder_here = jnp.where(keeps, holder, -1)
    base = SPAN * windows
    rows = blocks * windows
    intra = collect(2 * COLUMNS, COLUMNS)

    @pl.when(half == 0)
    def _():
        total[:, pl.ds(base, rows), :] = intra

    @pl.when(half == 1)
    def _():
        total[:, pl.ds(base + rows, rows), :] = intra
        total[:, pl.ds(base, rows), :] = collect(0, 2 * COLUMNS)

    for j in range(mine):
        out_ref[j] = total[j, pl.ds(me * windows + core * mine + j, base), :] * (1.0 / (chans * cores))

    for there, first, part, index in routes():
        @pl.when(there != me)
        def _():
            x_copy(there, first, part, index, me).wait_send()

    def sent(q, carry):
        part = jnp.where(inner, 0, q // blocks)
        i = lax.rem(q, blocks)
        far = jnp.logical_and(inner, q >= blocks)
        t = jnp.where(far, block(away, 1, i), block(here, 0, i))
        f_copy(t, part).wait_send()
        return carry

    lax.fori_loop(0, n, sent, 0)
    for local_t in range(blocks):
        @pl.when(target + local_t != me)
        def _():
            s_copy(local_t, holder).wait_send()
    e_copy.wait_send()


def spread_shards(spectra, offsets, channel_group):
    windows, chans, _, freq_bins = spectra.shape
    n = lax.axis_size("tm")
    cores = lax.axis_size("chan")
    blocks = n // 2
    groups = chans // windows
    band = SPAN * windows
    mine = windows // cores
    dma = pltpu.SemaphoreType.DMA
    tiles = (2 * (windows // PAIR), PAIR * windows, freq_bins)
    return pl.pallas_call(
        functools.partial(kernel, n, chans, windows, freq_bins, cores),
        out_shape=pltpu.VMEM((mine, band, LAGS), jnp.float32),
        in_specs=[
            pl.BlockSpec(memory_space=pl.ANY),
            pl.BlockSpec(memory_space=pltpu.SMEM),
            pl.BlockSpec(memory_space=pltpu.VMEM),
        ],
        out_specs=pl.BlockSpec(memory_space=pltpu.VMEM),
        scratch_shapes=[
            pltpu.VMEM((windows, 2 * chans, freq_bins), jnp.bfloat16),
            pltpu.VMEM((windows * 2 * chans, freq_bins), jnp.float32),
            pltpu.VMEM((windows * GROUPS, freq_bins), jnp.float32),
            pltpu.VMEM((windows, freq_bins), jnp.float32),
            pltpu.VMEM((windows, freq_bins), jnp.float32),
            pltpu.VMEM((groups,) + tiles, jnp.bfloat16),
            pltpu.VMEM((n, groups) + tiles, jnp.bfloat16),
            pltpu.VMEM((n, groups) + tiles, jnp.float32),
            pltpu.VMEM((2 * freq_bins, LAGS), jnp.bfloat16),
            pltpu.VMEM((blocks, mine, blocks * windows, LAGS), jnp.float32),
            pltpu.VMEM((mine, band + n * windows, LAGS), jnp.float32),
            pltpu.VMEM((blocks, mine, blocks * windows, LAGS), jnp.bfloat16),
            pltpu.VMEM((3 * COLUMNS, mine, blocks * windows, LAGS), jnp.bfloat16),
            dma, dma((2,)), dma, dma, dma((n,)), dma((n, 2)), dma((n, 2)), dma((n, 2)),
            dma((blocks,)), dma((3 * COLUMNS,)), pltpu.SemaphoreType.REGULAR((2,)),
        ],
        compiler_params=pltpu.CompilerParams(
            collective_id=0, has_side_effects=True, vmem_limit_bytes=56 * 1024 * 1024
        ),
    )(spectra.reshape(windows, 2 * chans, freq_bins), offsets, channel_group.reshape(1, chans))


def shards(spectra, offsets, channel_group):
    windows, chans, _, freq_bins = spectra.shape
    n = lax.axis_size("tm")
    fits = (
        chans == freq_bins == LAGS == 128
        and windows == 8
        and lax.axis_size("chan") == 2
        and n == 8
    )
    return (spread_shards if fits else ring_shards)(spectra, offsets, channel_group)


def solution(mesh):
    placed = (P(("arrays", "tm"), "chan", None, None), P(("arrays", "tm")), P(("arrays", "chan")))
    return jax.shard_map(
        shards,
        mesh=mesh,
        in_specs=placed,
        out_specs=P(("arrays", "tm", "chan"), None, None),
        check_vma=False,
    )
```

time: 38.9 us -> 35.7 us (0.918)
  the two profiles are of different devices: /device:TPU:11 before, /device:TPU:28 now
where the time goes in v1:
time: 35.7 us; the launch traced here: 35.6 us
  Pallas kernels  34.9 us (98%)
  local copies, waits for them, and re-layouts  0.64 us (2%)
    pallas_call x1, Pallas kernels, spread_shards(): pl.pallas_call(functools.partial(kernel, n, chans, windows, freq_bins, co...  34.9 us

profile of v1, /device:TPU:28, one launch (start us, length us, event | category | flops | bytes accessed | tf_op | source)
XLA Modules:
  0.0 35.6 jit_solution(172611704192331702)
XLA Ops:
  0.0 34.9 %shard_map.37 = f32[4,48,128]{2,1,0:T(8,128)S(1)} custom-call(bf16[8,256,128]{2,1,0:T(8,128)(2,1)} %bitcast.2, s32[8]{0:T(128)} %off_ref.1, s32[1,128]{1,0:T(1,128)} %bitcast.3), custom_call_target="tpu_custom_call" | custom-call | tf_op jit(solution)/shard_map/pallas_call | solution.py:450
  34.9 0.6 %copy.5 = f32[4,48,128]{2,1,0:T(8,128)} copy(f32[4,48,128]{2,1,0:T(8,128)S(1)} %shard_map.37) | data formatting | bytes 196608

commit v2 on v1

v2 whole, which is shorter than its diff:
```python
import functools
import math

import jax
import jax.numpy as jnp
from jax import lax
from jax.experimental import pallas as pl
from jax.experimental.pallas import tpu as pltpu
from jax.sharding import PartitionSpec as P

LAGS = 128
GROUPS = 8
SPAN = 6


epsilon = 1e-05


def shifted(value, axis, steps):
    count = lax.axis_size(axis)
    initial, last = (max(0, -steps), min(count, count - steps))
    return lax.ppermute(value, axis, [(source, source + steps) for source in range(initial, last)])


def lag_table(freq_bins, lag_count):
    frequency = jnp.arange(freq_bins, dtype=jnp.int32)[:, None]
    lag_shift = jnp.arange(lag_count, dtype=jnp.int32)[None, :] - lag_count // 2
    phase_turns = jnp.mod(frequency * lag_shift, 2 * freq_bins).astype(jnp.float32)
    phase_angle = jnp.pi * phase_turns / freq_bins
    normaliser = 1.0 / math.sqrt(freq_bins)
    lag_rows = jnp.concatenate(
        [jnp.cos(phase_angle) * normaliser, -jnp.sin(phase_angle) * normaliser], axis=0
    )
    return lag_rows.astype(jnp.bfloat16)


def align_spectra(spectra, offsets, scales):
    freq_bins = spectra.shape[3]
    frequency = jnp.arange(freq_bins, dtype=jnp.int32)[None, :]
    phase_turns = jnp.mod(offsets[:, None] * frequency, 2 * freq_bins).astype(jnp.float32)
    phase_angle = jnp.pi * phase_turns / freq_bins
    cosine = jnp.cos(phase_angle)[:, None, :]
    sine_part = jnp.sin(phase_angle)[:, None, :]
    real_part = spectra[:, :, 0, :].astype(jnp.float32)
    imag_part = spectra[:, :, 1, :].astype(jnp.float32)
    weight = scales[:, :, None]
    out_real = weight * (real_part * cosine + imag_part * sine_part)
    out_imag = weight * (imag_part * cosine - real_part * sine_part)
    return jnp.stack([out_real, out_imag], axis=2).astype(jnp.bfloat16)


def window_terms(current, band_rows, lag_rows):
    left_real = current[None, :, 0, :].astype(jnp.float32)
    left_imag = current[None, :, 1, :].astype(jnp.float32)
    right_real = band_rows[:, :, 0, :].astype(jnp.float32)
    right_imag = band_rows[:, :, 1, :].astype(jnp.float32)
    prod_real = left_real * right_real + left_imag * right_imag
    prod_imag = left_imag * right_real - left_real * right_imag
    cross_spec = jnp.stack([prod_real, prod_imag], axis=2).astype(jnp.bfloat16)
    flattened = cross_spec.reshape(band_rows.shape[0] * band_rows.shape[1], 2 * band_rows.shape[3])
    lagged = jnp.dot(flattened, lag_rows, preferred_element_type=jnp.float32)
    lagged = lagged.reshape(band_rows.shape[0], band_rows.shape[1], lag_rows.shape[1])
    return jnp.sum(lagged * lagged, axis=1)


def ring_shards(spectra, offsets, channel_group):
    windows = spectra.shape[0]
    local_chans = spectra.shape[1]
    freq_bins = spectra.shape[3]
    chan_count = lax.axis_size("chan")
    channels = local_chans * chan_count
    onehot = (channel_group[:, None] == jnp.arange(GROUPS, dtype=jnp.int32)[None, :]).astype(
        jnp.float32
    )
    chan_power = jnp.sum(jnp.square(spectra.astype(jnp.float32)), axis=(2, 3))
    partial_value = jnp.dot(chan_power, onehot, precision=lax.Precision.HIGHEST)
    group_total = lax.psum(partial_value, "chan")
    energy = group_total * (GROUPS / (freq_bins * channels))
    scales = jnp.dot(lax.rsqrt(energy + epsilon), onehot.T, precision=lax.Precision.HIGHEST)
    aligned = align_spectra(spectra, offsets, scales)
    earlier = []
    carried = aligned
    for distance in range(SPAN):
        carried = shifted(carried, "tm", 1)
        earlier.append(carried)
    buffer = jnp.concatenate(earlier[::-1] + [aligned], axis=0)
    lag_rows = lag_table(freq_bins, LAGS)
    band_len = SPAN * windows

    def one_window(window):
        current = lax.dynamic_index_in_dim(aligned, window, 0, keepdims=False)
        band_rows = lax.dynamic_slice_in_dim(buffer, window, band_len, 0)
        return window_terms(current, band_rows, lag_rows) * (1.0 / channels)

    return lax.psum_scatter(
        lax.map(
            one_window, jnp.arange(lax.axis_size("chan") * (windows // chan_count), dtype=jnp.int32)
        ).astype(jnp.bfloat16),
        "chan",
        scatter_dimension=0,
        tiled=True,
    ).astype(jnp.float32)


HIGHEST = lax.Precision.HIGHEST
ROWS = 16
COLUMNS = 2
PARTS = 4
FAR = 2


def phase_of(turns, freq_bins):
    period = 2.0 * freq_bins
    return (jnp.pi / freq_bins) * (turns - period * jnp.floor(turns / period))


def kernel(
    n, chans, windows, freq_bins, cores,
    x_ref, off_ref, group_ref, out_ref,
    local, wide, sums, tile, tile_in, al, right, left, table, acc, total, sum_out, sum_in,
    local_sem, own_sem, e_send, e_recv, x_send, x_recv, s_send, s_recv, ready,
):
    me = lax.axis_index("tm")
    core = lax.axis_index("chan")
    levels = n // COLUMNS
    level, column = me // COLUMNS, lax.rem(me, COLUMNS)
    half = level // 2
    inner = jnp.logical_or(level == 1, level == levels - 2)
    blocks = n // 2
    mine = windows // cores
    lanes = freq_bins
    bf16 = jnp.bfloat16
    share = chans // PARTS
    tiles = share // ROWS
    mesh_id = pl.DeviceIdType.MESH

    loads = [pltpu.make_async_copy(x_ref.at[w], local.at[w], local_sem.at[w]) for w in range(windows)]
    for load in loads:
        load.start()

    barrier = pltpu.get_barrier_semaphore()
    beside = COLUMNS * level + 1 - column
    above, below = level + 1 < levels, level > 0

    def greet(sem):
        pl.semaphore_signal(sem, inc=1, device_id={"tm": beside}, device_id_type=mesh_id)

        @pl.when(above)
        def _():
            pl.semaphore_signal(sem, inc=1, device_id={"tm": me + COLUMNS}, device_id_type=mesh_id)

        @pl.when(below)
        def _():
            pl.semaphore_signal(sem, inc=1, device_id={"tm": me - COLUMNS}, device_id_type=mesh_id)

    near = 1 + jnp.where(above, 1, 0) + jnp.where(below, 1, 0)
    pl.semaphore_signal(barrier, inc=1, device_id={"chan": 1 - core}, device_id_type=mesh_id)
    greet(barrier)

    frequency = lax.broadcasted_iota(jnp.int32, (freq_bins, LAGS), 0)
    shift = lax.broadcasted_iota(jnp.int32, (freq_bins, LAGS), 1) - LAGS // 2
    group_id = lax.broadcasted_iota(jnp.int32, (GROUPS, chans), 0)
    onehot = (group_id == group_ref[...]).astype(jnp.float32)
    few = onehot.astype(bf16)
    both = jnp.concatenate([few, few], axis=1)
    member = jnp.concatenate([few, few, few, few], axis=0)
    lane = lax.broadcasted_iota(jnp.int32, (windows, lanes), 1)
    row = lax.broadcasted_iota(jnp.int32, (windows, lanes), 0)

    for w in range(windows):
        loads[w].wait()
        if w == windows - 1:
            pl.semaphore_wait(barrier, near + 1)
            greet(ready.at[0])
        wide[pl.ds(w * 2 * chans, 2 * chans), :] = local[w].astype(jnp.float32)
        real = wide[pl.ds(w * 2 * chans, chans, stride=2), :]
        imag = wide[pl.ds(w * 2 * chans + 1, chans, stride=2), :]
        power = real * real + imag * imag
        high = power.astype(bf16)
        low = (power - high.astype(jnp.float32)).astype(bf16)
        sums[pl.ds(w * GROUPS, GROUPS), :] = jnp.dot(
            both, jnp.concatenate([high, low], axis=0), preferred_element_type=jnp.float32
        )
    totals = jnp.broadcast_to(jnp.sum(sums[...], axis=1, keepdims=True), sums.shape)
    tile[...] = totals
    e_copy = pltpu.make_async_remote_copy(
        src_ref=tile, dst_ref=tile_in, send_sem=e_send, recv_sem=e_recv,
        device_id={"chan": 1 - core}, device_id_type=mesh_id,
    )
    e_copy.start()

    angle = phase_of((frequency * shift).astype(jnp.float32), freq_bins)
    normaliser = 1.0 / math.sqrt(freq_bins)
    table[pl.ds(0, freq_bins), :] = (jnp.cos(angle) * normaliser).astype(bf16)
    table[pl.ds(freq_bins, freq_bins), :] = (-jnp.sin(angle) * normaliser).astype(bf16)
    starts = jnp.zeros((windows, lanes), jnp.float32)
    for w in range(windows):
        starts = jnp.where(row == w, off_ref[w].astype(jnp.float32), starts)
    theta = phase_of(lane.astype(jnp.float32) * starts, freq_bins)
    cosine = jnp.cos(theta)
    sine = jnp.sin(theta)
    acc[...] = jnp.zeros_like(acc)
    total[:, pl.ds(0, SPAN * windows), :] = jnp.zeros((mine, SPAN * windows, LAGS), jnp.float32)

    pl.semaphore_wait(ready.at[0], near)
    greet(ready.at[1])
    e_copy.wait_recv()
    energy = (totals + tile_in[...]) * (GROUPS / (freq_bins * chans * cores))
    scales = lax.rsqrt(energy + epsilon)

    for w in range(windows):
        factor = scales[w * GROUPS : (w + 1) * GROUPS]
        turn = jnp.concatenate([factor * cosine[w : w + 1], factor * sine[w : w + 1]], axis=1)
        top = turn.astype(bf16)
        rest = turn - top.astype(jnp.float32)
        middle = rest.astype(bf16)
        bottom = (rest - middle.astype(jnp.float32)).astype(bf16)
        pieces = jnp.concatenate([top, middle, bottom, jnp.zeros_like(top)], axis=0)
        factors = lax.dot_general(
            member, pieces, (((0,), (0,)), ((), ())), preferred_element_type=jnp.float32
        )
        real = wide[pl.ds(w * 2 * chans, chans, stride=2), :]
        imag = wide[pl.ds(w * 2 * chans + 1, chans, stride=2), :]
        turn_cos, turn_sin = factors[:, :lanes], factors[:, lanes:]
        out = (real * turn_cos + imag * turn_sin, imag * turn_cos - real * turn_sin)
        for r in range(2):
            al[:, w, :, r] = out[r].astype(bf16).reshape(PARTS, tiles, ROWS, freq_bins)

    def routes():
        def inside(own, flip):
            place = COLUMNS * (half if own else 1 - half) + lax.rem(column + core + flip, 2)
            return COLUMNS + place, place, 0, 2 * (1 - own) + flip

        yield inside(1, 0)
        yield inside(0, 0)
        yield inside(0, 1)
        yield inside(1, 1)
        for part in range(2):
            for flip in range(COLUMNS):
                place = lax.rem(column + core + flip, 2)
                yield (n - COLUMNS) * half + place, 2 * place + part, part, 4 + 2 * part + flip

    def x_copy(there, first, part, index, source):
        return pltpu.make_async_remote_copy(
            src_ref=al.at[first],
            dst_ref=right.at[source, part],
            send_sem=x_send.at[index],
            recv_sem=x_recv.at[source, part],
            device_id={"tm": there},
            device_id_type=mesh_id,
        )

    def own_copy(first, part):
        return pltpu.make_async_copy(al.at[first], right.at[me, part], own_sem.at[part])

    for there, first, part, index in routes():
        if index == FAR:
            @pl.when(jnp.logical_not(inner))
            def _():
                pl.semaphore_wait(ready.at[1], near)

        @pl.when(there == me)
        def _():
            own_copy(first, part).start()

        @pl.when(there != me)
        def _():
            x_copy(there, first, part, index, me).start()

    @pl.when(inner)
    def _():
        pl.semaphore_wait(ready.at[1], near)

    greet(ready.at[2])

    bit = lax.rem(level, 2)

    def block(base, flip, k):
        turned = core * jnp.maximum(flip, k // 2)
        return base + COLUMNS * lax.rem(bit + flip + k // 2, 2) + lax.rem(column + turned + lax.rem(k, 2), 2)

    here, away = blocks * half, blocks * (1 - half)

    def job(sets, part):
        for w in range(windows):
            rows = []
            for upper, lower in sets:
                for i in range(tiles):
                    left_real = left[upper, part, w, i, 0].astype(bf16)
                    left_imag = left[upper, part, w, i, 1].astype(bf16)
                    for v in range(windows):
                        right_real = right[lower, part, v, i, 0]
                        right_imag = right[lower, part, v, i, 1]
                        rows.append(
                            jnp.concatenate(
                                [
                                    left_real * right_real + left_imag * right_imag,
                                    left_imag * right_real - left_real * right_imag,
                                ],
                                axis=1,
                            )
                        )
            lagged = jnp.dot(jnp.concatenate(rows, axis=0), table[...], preferred_element_type=jnp.float32)
            lagged = lagged.reshape(len(sets), tiles, windows, ROWS // 8, 8, LAGS)
            squares = jnp.sum(lagged * lagged, axis=(1, 3))
            for k, (upper, lower) in enumerate(sets):
                up, low = lax.rem(upper, blocks), lax.rem(lower, blocks)
                acc[up, w, pl.ds(low * windows * 8, windows * 8), :] += squares[k].reshape(windows * 8, LAGS)

    holder = cores * jnp.where(inner, me - COLUMNS, 2 * COLUMNS + column) + core
    crossing, holders = 2 * COLUMNS * cores, 3 * COLUMNS * cores

    def s_copy(up, low, k, there, source):
        return pltpu.make_async_remote_copy(
            src_ref=sum_out.at[up, low, k],
            dst_ref=sum_in.at[source, low],
            send_sem=s_send.at[up, low, k],
            recv_sem=s_recv.at[source, low],
            device_id={"tm": there, "chan": k},
            device_id_type=mesh_id,
        )

    def hand_over(upper, lower):
        up, low = lax.rem(upper, blocks), lax.rem(lower, blocks)
        for k in range(cores):
            result = []
            for j in range(mine):
                held = [
                    acc[up, k * mine + j, pl.ds(low * windows * 8 + i, windows, stride=8), :] for i in range(8)
                ]
                while len(held) > 1:
                    held = [one + two for one, two in zip(held[::2], held[1::2])]
                result.append(held[0])
            sum_out[up, low, k] = jnp.stack(result, axis=0).astype(bf16)

            @pl.when(jnp.logical_or(upper != me, core != k))
            def _():
                s_copy(up, low, k, upper, holder).start()

            @pl.when(jnp.logical_and(upper == me, core == k))
            def _():
                sum_in[holder, low] = sum_out[up, low, k]

    def place_of(q):
        part = jnp.where(inner, 0, q // blocks)
        i = lax.rem(q, blocks)
        far = jnp.logical_and(inner, q >= blocks)
        t = jnp.where(far, block(away, 1, i), block(here, 0, i))
        count = jnp.where(inner, jnp.where(far, blocks, 0), i + 1)
        done = jnp.where(jnp.logical_or(inner, part == 1), count, 0)
        return t, part, count, done

    def ordered(t, k):
        other = block(here, 0, k)
        return jnp.maximum(t, other), jnp.minimum(t, other)

    def step(q, carry):
        t, part, count, done = place_of(q)

        @pl.when(t == me)
        def _():
            own_copy(0, part).wait()

        @pl.when(t != me)
        def _():
            x_copy(me, 0, part, 0, t).wait_recv()

        left[t, part] = right[t, part].astype(jnp.float32)

        def two_jobs(k, inside):
            job([ordered(t, 2 * k), ordered(t, 2 * k + 1)], part)
            return inside

        lax.fori_loop(0, count // 2, two_jobs, 0)

        @pl.when(lax.rem(count, 2) == 1)
        def _():
            job([ordered(t, count - 1)], part)

        @pl.when(q == blocks)
        def _():
            pl.semaphore_wait(ready.at[2], near)

        def one_block(k, inside):
            hand_over(*ordered(t, k))
            return inside

        lax.fori_loop(0, done, one_block, 0)
        return carry

    lax.fori_loop(0, n, step, 0)

    def collect(first, last, low):
        result = None
        for source in range(first, last):
            @pl.when(jnp.logical_or(source != holder, jnp.logical_not(keeps)))
            def _():
                s_copy(0, low, 0, me, source).wait_recv()

            value = sum_in[source, low].astype(jnp.float32)
            result = value if result is None else result + value
        return result

    target = blocks * jnp.where(inner, 1, half)
    keeps = jnp.logical_and(me >= target, me < target + blocks)
    base = SPAN * windows
    for low in range(blocks):
        @pl.when(half == 1)
        def _():
            total[:, pl.ds(base + low * windows, windows), :] = collect(0, crossing, low)

        @pl.when(low <= lax.rem(me, blocks))
        def _():
            total[:, pl.ds(base + (blocks * half + low) * windows, windows), :] = collect(crossing, holders, low)

    for j in range(mine):
        out_ref[j] = total[j, pl.ds(me * windows + core * mine + j, base), :] * (1.0 / (chans * cores))

    for there, first, part, index in routes():
        @pl.when(there != me)
        def _():
            x_copy(there, first, part, index, me).wait_send()

    def sent(q, carry):
        t, _, _, done = place_of(q)

        def one_block(k, inside):
            upper, lower = ordered(t, k)
            for c in range(cores):
                @pl.when(jnp.logical_or(upper != me, core != c))
                def _():
                    s_copy(lax.rem(upper, blocks), lax.rem(lower, blocks), c, upper, holder).wait_send()

            return inside

        lax.fori_loop(0, done, one_block, 0)
        return carry

    lax.fori_loop(0, n, sent, 0)
    e_copy.wait_send()


def spread_shards(spectra, offsets, channel_group):
    windows, chans, _, freq_bins = spectra.shape
    n = lax.axis_size("tm")
    cores = lax.axis_size("chan")
    blocks = n // 2
    band = SPAN * windows
    mine = windows // cores
    dma = pltpu.SemaphoreType.DMA
    pieces = (windows, chans // PARTS // ROWS, 2, ROWS, freq_bins)
    return pl.pallas_call(
        functools.partial(kernel, n, chans, windows, freq_bins, cores),
        out_shape=pltpu.VMEM((mine, band, LAGS), jnp.float32),
        in_specs=[
            pl.BlockSpec(memory_space=pl.ANY),
            pl.BlockSpec(memory_space=pltpu.SMEM),
            pl.BlockSpec(memory_space=pltpu.VMEM),
        ],
        out_specs=pl.BlockSpec(memory_space=pltpu.VMEM),
        scratch_shapes=[
            pltpu.VMEM((windows, 2 * chans, freq_bins), jnp.bfloat16),
            pltpu.VMEM((windows * 2 * chans, freq_bins), jnp.float32),
            pltpu.VMEM((windows * GROUPS, freq_bins), jnp.float32),
            pltpu.VMEM((windows * GROUPS, freq_bins), jnp.float32),
            pltpu.VMEM((windows * GROUPS, freq_bins), jnp.float32),
            pltpu.VMEM((PARTS,) + pieces, jnp.bfloat16),
            pltpu.VMEM((n, 2) + pieces, jnp.bfloat16),
            pltpu.VMEM((n, 2) + pieces, jnp.float32),
            pltpu.VMEM((2 * freq_bins, LAGS), jnp.bfloat16),
            pltpu.VMEM((blocks, windows, blocks * windows * 8, LAGS), jnp.float32),
            pltpu.VMEM((mine, band + n * windows, LAGS), jnp.float32),
            pltpu.VMEM((blocks, blocks, cores, mine, windows, LAGS), jnp.bfloat16),
            pltpu.VMEM((3 * COLUMNS * cores, blocks, mine, windows, LAGS), jnp.bfloat16),
            dma((windows,)), dma((2,)), dma, dma, dma((n,)), dma((n, 2)),
            dma((blocks, blocks, cores)), dma((3 * COLUMNS * cores, blocks)), pltpu.SemaphoreType.REGULAR((3,)),
        ],
        compiler_params=pltpu.CompilerParams(
            collective_id=0, has_side_effects=True, vmem_limit_bytes=56 * 1024 * 1024
        ),
    )(spectra.reshape(windows, 2 * chans, freq_bins), offsets, channel_group.reshape(1, chans))


def shards(spectra, offsets, channel_group):
    windows, chans, _, freq_bins = spectra.shape
    n = lax.axis_size("tm")
    fits = (
        chans == freq_bins == LAGS == 128
        and windows == 8
        and lax.axis_size("chan") == 2
        and n == 8
    )
    return (spread_shards if fits else ring_shards)(spectra, offsets, channel_group)


def solution(mesh):
    placed = (P(("arrays", "tm"), "chan", None, None), P(("arrays", "tm")), P(("arrays", "chan")))
    return jax.shard_map(
        shards,
        mesh=mesh,
        in_specs=placed,
        out_specs=P(("arrays", "tm", "chan"), None, None),
        check_vma=False,
    )
```

time: 35.7 us -> 31.7 us (0.89)
  Pallas kernels: 34.9 us -> 30.6 us
    pallas_call x1, Pallas kernels: 34.9 us -> 30.6 us  [spread_shards(): pl.pallas_call(functools.partial(kernel, n, chans, windows, freq_bins, co...]
where the time goes in v2:
time: 31.7 us; the launch traced here: 31.2 us
  Pallas kernels  30.6 us (97%)
  local copies, waits for them, and re-layouts  0.64 us (2%)
    pallas_call x1, Pallas kernels, spread_shards(): pl.pallas_call(functools.partial(kernel, n, chans, windows, freq_bins, co...  30.6 us
    unnamed x1, local copies, waits for them, and re-layouts  0.64 us

profile of v2, /device:TPU:28, one launch (start us, length us, event | category | flops | bytes accessed | tf_op | source)
XLA Modules:
  0.0 31.2 jit_solution(1377350169153077165)
XLA Ops:
  0.0 30.6 %shard_map.37 = f32[4,48,128]{2,1,0:T(8,128)S(1)} custom-call(bf16[8,256,128]{2,1,0:T(8,128)(2,1)} %bitcast.2, s32[8]{0:T(128)} %off_ref.1, s32[1,128]{1,0:T(1,128)} %bitcast.3), custom_call_target="tpu_custom_call" | custom-call | tf_op jit(solution)/shard_map/pallas_call | solution.py:452
  30.6 0.6 %copy.5 = f32[4,48,128]{2,1,0:T(8,128)} copy(f32[4,48,128]{2,1,0:T(8,128)S(1)} %shard_map.37) | data formatting | bytes 196608

commit v3 on v2

--- a/solution.py
+++ b/solution.py
@@ -116,9 +116,9 @@
 
 def kernel(
     n, chans, windows, freq_bins, cores,
-    x_ref, off_ref, group_ref, out_ref,
-    local, wide, sums, tile, tile_in, al, right, left, table, acc, total, sum_out, sum_in,
-    local_sem, own_sem, e_send, e_recv, x_send, x_recv, s_send, s_recv, ready,
+    x_ref, off_hbm, group_hbm, out_ref,
+    off_ref, group_ref, local, wide, sums, tile, tile_in, al, right, left, table, acc, total, sum_out, sum_in,
+    small_sem, local_sem, own_sem, e_send, e_recv, x_send, x_recv, s_send, s_recv, ready,
 ):
     me = lax.axis_index("tm")
     core = lax.axis_index("chan")
@@ -153,10 +153,17 @@
         def _():
             pl.semaphore_signal(sem, inc=1, device_id={"tm": me - COLUMNS}, device_id_type=mesh_id)
 
+    small = [
+        pltpu.make_async_copy(group_hbm, group_ref, small_sem.at[0]),
+        pltpu.make_async_copy(off_hbm, off_ref, small_sem.at[1]),
+    ]
+    for copy in small:
+        copy.start()
     near = 1 + jnp.where(above, 1, 0) + jnp.where(below, 1, 0)
     pl.semaphore_signal(barrier, inc=1, device_id={"chan": 1 - core}, device_id_type=mesh_id)
     greet(barrier)
 
+    small[0].wait()
     frequency = lax.broadcasted_iota(jnp.int32, (freq_bins, LAGS), 0)
     shift = lax.broadcasted_iota(jnp.int32, (freq_bins, LAGS), 1) - LAGS // 2
     group_id = lax.broadcasted_iota(jnp.int32, (GROUPS, chans), 0)
@@ -193,6 +200,7 @@
     normaliser = 1.0 / math.sqrt(freq_bins)
     table[pl.ds(0, freq_bins), :] = (jnp.cos(angle) * normaliser).astype(bf16)
     table[pl.ds(freq_bins, freq_bins), :] = (-jnp.sin(angle) * normaliser).astype(bf16)
+    small[1].wait()
     starts = jnp.zeros((windows, lanes), jnp.float32)
     for w in range(windows):
         starts = jnp.where(row == w, off_ref[w].astype(jnp.float32), starts)
@@ -232,9 +240,9 @@
             return COLUMNS + place, place, 0, 2 * (1 - own) + flip
 
         yield inside(1, 0)
+        yield inside(1, 1)
         yield inside(0, 0)
         yield inside(0, 1)
-        yield inside(1, 1)
         for part in range(2):
             for flip in range(COLUMNS):
                 place = lax.rem(column + core + flip, 2)
@@ -367,25 +375,34 @@
 
         left[t, part] = right[t, part].astype(jnp.float32)
 
+        @pl.when(q == 1)
+        def _():
+            pl.semaphore_wait(ready.at[2], near)
+
+        finished = done > 0
+
         def two_jobs(k, inside):
-            job([ordered(t, 2 * k), ordered(t, 2 * k + 1)], part)
+            sets = [ordered(t, 2 * k), ordered(t, 2 * k + 1)]
+            job(sets, part)
+
+            @pl.when(finished)
+            def _():
+                for upper, lower in sets:
+                    hand_over(upper, lower)
+
             return inside
 
         lax.fori_loop(0, count // 2, two_jobs, 0)
 
         @pl.when(lax.rem(count, 2) == 1)
         def _():
-            job([ordered(t, count - 1)], part)
-
-        @pl.when(q == blocks)
-        def _():
-            pl.semaphore_wait(ready.at[2], near)
-
-        def one_block(k, inside):
-            hand_over(*ordered(t, k))
-            return inside
-
-        lax.fori_loop(0, done, one_block, 0)
+            upper, lower = ordered(t, count - 1)
+            job([(upper, lower)], part)
+
+            @pl.when(finished)
+            def _():
+                hand_over(upper, lower)
+
         return carry
 
     lax.fori_loop(0, n, step, 0)
@@ -454,11 +471,13 @@
         out_shape=pltpu.VMEM((mine, band, LAGS), jnp.float32),
         in_specs=[
             pl.BlockSpec(memory_space=pl.ANY),
-            pl.BlockSpec(memory_space=pltpu.SMEM),
-            pl.BlockSpec(memory_space=pltpu.VMEM),
+            pl.BlockSpec(memory_space=pl.ANY),
+            pl.BlockSpec(memory_space=pl.ANY),
         ],
         out_specs=pl.BlockSpec(memory_space=pltpu.VMEM),
         scratch_shapes=[
+            pltpu.SMEM((windows,), jnp.int32),
+            pltpu.VMEM((1, chans), jnp.int32),
             pltpu.VMEM((windows, 2 * chans, freq_bins), jnp.bfloat16),
             pltpu.VMEM((windows * 2 * chans, freq_bins), jnp.float32),
             pltpu.VMEM((windows * GROUPS, freq_bins), jnp.float32),
@@ -472,7 +491,7 @@
             pltpu.VMEM((mine, band + n * windows, LAGS), jnp.float32),
             pltpu.VMEM((blocks, blocks, cores, mine, windows, LAGS), jnp.bfloat16),
             pltpu.VMEM((3 * COLUMNS * cores, blocks, mine, windows, LAGS), jnp.bfloat16),
-            dma((windows,)), dma((2,)), dma, dma, dma((n,)), dma((n, 2)),
+            dma((2,)), dma((windows,)), dma((2,)), dma, dma, dma((n,)), dma((n, 2)),
             dma((blocks, blocks, cores)), dma((3 * COLUMNS * cores, blocks)), pltpu.SemaphoreType.REGULAR((3,)),
         ],
         compiler_params=pltpu.CompilerParams(

time: 31.7 us -> 28.7 us (0.905)
  Pallas kernels: 30.6 us -> 27.6 us
    pallas_call x1, Pallas kernels: 30.6 us -> 27.6 us  [spread_shards(): pl.pallas_call(functools.partial(kernel, n, chans, windows, freq_bins, co...]
where the time goes in v3:
time: 28.7 us; the launch traced here: 28.3 us
  Pallas kernels  27.6 us (96%)
  local copies, waits for them, and re-layouts  0.64 us (2%)
    pallas_call x1, Pallas kernels, spread_shards(): pl.pallas_call(functools.partial(kernel, n, chans, windows, freq_bins, co...  27.6 us
    unnamed x1, local copies, waits for them, and re-layouts  0.64 us

profile of v3, /device:TPU:28, one launch (start us, length us, event | category | flops | bytes accessed | tf_op | source)
XLA Modules:
  0.0 28.3 jit_solution(8574898923799348709)
XLA Ops:
  0.0 27.6 %shard_map.37 = f32[4,48,128]{2,1,0:T(8,128)S(1)} custom-call(bf16[8,256,128]{2,1,0:T(8,128)(2,1)} %bitcast.2, s32[8]{0:T(128)} %off_hbm.1, s32[1,128]{1,0:T(1,128)} %bitcast.3), custom_call_target="tpu_custom_call" | custom-call | tf_op jit(solution)/shard_map/pallas_call | solution.py:469
  27.6 0.6 %copy.5 = f32[4,48,128]{2,1,0:T(8,128)} copy(f32[4,48,128]{2,1,0:T(8,128)S(1)} %shard_map.37) | data formatting | bytes 196608

commit v4 on v3

--- a/solution.py
+++ b/solution.py
@@ -104,9 +104,9 @@
 
 HIGHEST = lax.Precision.HIGHEST
 ROWS = 16
+FAR = 2
 COLUMNS = 2
 PARTS = 4
-FAR = 2
 
 
 def phase_of(turns, freq_bins):
@@ -261,19 +261,30 @@
     def own_copy(first, part):
         return pltpu.make_async_copy(al.at[first], right.at[me, part], own_sem.at[part])
 
-    for there, first, part, index in routes():
-        if index == FAR:
-            @pl.when(jnp.logical_not(inner))
-            def _():
+    ways = list(routes())
+
+    def send(index):
+        there, first, part, index = ways[index]
+
+        @pl.when(there == me)
+        def _():
+            own_copy(first, part).start()
+
+        @pl.when(there != me)
+        def _():
+            x_copy(there, first, part, index, me).start()
+
+    @pl.when(inner)
+    def _():
+        for index in (0, 1, 4, 5, 6, 7, 2, 3):
+            send(index)
+
+    @pl.when(jnp.logical_not(inner))
+    def _():
+        for index in (0, 1, 4, 5, 6, 7, 2, 3):
+            if index == FAR:
                 pl.semaphore_wait(ready.at[1], near)
-
-        @pl.when(there == me)
-        def _():
-            own_copy(first, part).start()
-
-        @pl.when(there != me)
-        def _():
-            x_copy(there, first, part, index, me).start()
+            send(index)
 
     @pl.when(inner)
     def _():
@@ -422,18 +433,24 @@
     keeps = jnp.logical_and(me >= target, me < target + blocks)
     base = SPAN * windows
     for low in range(blocks):
+        @pl.when(low <= lax.rem(me, blocks))
+        def _():
+            total[:, pl.ds(base + (blocks * half + low) * windows, windows), :] = collect(crossing, holders, low)
+
+    for low in range(blocks):
         @pl.when(half == 1)
         def _():
-            total[:, pl.ds(base + low * windows, windows), :] = collect(0, crossing, low)
-
-        @pl.when(low <= lax.rem(me, blocks))
-        def _():
-            total[:, pl.ds(base + (blocks * half + low) * windows, windows), :] = collect(crossing, holders, low)
+            total[:, pl.ds(base + low * windows, windows), :] = collect(crossing // 2, crossing, low)
+
+    for low in range(blocks):
+        @pl.when(half == 1)
+        def _():
+            total[:, pl.ds(base + low * windows, windows), :] += collect(0, crossing // 2, low)
 
     for j in range(mine):
         out_ref[j] = total[j, pl.ds(me * windows + core * mine + j, base), :] * (1.0 / (chans * cores))
 
-    for there, first, part, index in routes():
+    for there, first, part, index in ways:
         @pl.when(there != me)
         def _():
             x_copy(there, first, part, index, me).wait_send()

time: 28.7 us -> 28.6 us (level)
  no operation moved by 1% of the time
where the time goes in v4:
time: 28.6 us; the launch traced here: 28.2 us
  Pallas kernels  27.5 us (96%)
  local copies, waits for them, and re-layouts  0.64 us (2%)
    pallas_call x1, Pallas kernels, spread_shards(): pl.pallas_call(functools.partial(kernel, n, chans, windows, freq_bins, co...  27.5 us
    unnamed x1, local copies, waits for them, and re-layouts  0.64 us

profile of v4, /device:TPU:28, one launch (start us, length us, event | category | flops | bytes accessed | tf_op | source)
XLA Modules:
  0.0 28.2 jit_solution(7960623422079465046)
XLA Ops:
  0.0 27.5 %shard_map.37 = f32[4,48,128]{2,1,0:T(8,128)S(1)} custom-call(bf16[8,256,128]{2,1,0:T(8,128)(2,1)} %bitcast.2, s32[8]{0:T(128)} %off_hbm.1, s32[1,128]{1,0:T(1,128)} %bitcast.3), custom_call_target="tpu_custom_call" | custom-call | tf_op jit(solution)/shard_map/pallas_call | solution.py:486
  27.5 0.6 %copy.5 = f32[4,48,128]{2,1,0:T(8,128)} copy(f32[4,48,128]{2,1,0:T(8,128)S(1)} %shard_map.37) | data formatting | bytes 196608

commit v5 on v4

--- a/solution.py
+++ b/solution.py
@@ -364,7 +364,7 @@
         part = jnp.where(inner, 0, q // blocks)
         i = lax.rem(q, blocks)
         far = jnp.logical_and(inner, q >= blocks)
-        t = jnp.where(far, block(away, 1, i), block(here, 0, i))
+        t = jnp.where(far, block(away, 1, 2 * lax.rem(i, 2) + i // 2), block(here, 0, i))
         count = jnp.where(inner, jnp.where(far, blocks, 0), i + 1)
         done = jnp.where(jnp.logical_or(inner, part == 1), count, 0)
         return t, part, count, done

time: 28.6 us -> 28.3 us (0.990)
  Pallas kernels: 27.5 us -> 27.2 us
    pallas_call x1, Pallas kernels: 27.5 us -> 27.2 us  [spread_shards(): pl.pallas_call(functools.partial(kernel, n, chans, windows, freq_bins, co...]
where the time goes in v5:
time: 28.3 us; the launch traced here: 27.9 us
  Pallas kernels  27.2 us (96%)
  local copies, waits for them, and re-layouts  0.64 us (2%)
    pallas_call x1, Pallas kernels, spread_shards(): pl.pallas_call(functools.partial(kernel, n, chans, windows, freq_bins, co...  27.2 us
    unnamed x1, local copies, waits for them, and re-layouts  0.64 us

profile of v5, /device:TPU:28, one launch (start us, length us, event | category | flops | bytes accessed | tf_op | source)
XLA Modules:
  0.0 27.9 jit_solution(1625818226417609081)
XLA Ops:
  0.0 27.2 %shard_map.37 = f32[4,48,128]{2,1,0:T(8,128)S(1)} custom-call(bf16[8,256,128]{2,1,0:T(8,128)(2,1)} %bitcast.2, s32[8]{0:T(128)} %off_hbm.1, s32[1,128]{1,0:T(1,128)} %bitcast.3), custom_call_target="tpu_custom_call" | custom-call | tf_op jit(solution)/shard_map/pallas_call | solution.py:486
  27.2 0.6 %copy.5 = f32[4,48,128]{2,1,0:T(8,128)} copy(f32[4,48,128]{2,1,0:T(8,128)S(1)} %shard_map.37) | data formatting | bytes 196608
